TPU v7x, 32 devices: a whole 2x2x4 slice. The times are simulated.
32 devices in a mesh: energy: 8 (over z, y), mom: 4 (over x, core).
Axes of the slice: x: 2, y: 2, z: 4, core: 2. Of those that a mesh axis runs over, the one named last changes fastest.
Arguments:
- green_ret: bfloat16 [16, 16, 2, 512, 512], P('mom', 'energy'), may hold values from -0.25 to 0.25
- broadening: float32 [16, 16, 512], P('mom', 'energy'), may hold values from 0.2 to 2
- coupling: bfloat16 [16, 512, 512], P(None, 'mom'), may hold values from -1.5 to 1.5
- shift_steps: int32 [4], replicated, may hold values from 1 to 2, as said below
- mode_weight: float32 [4], replicated, may hold values from 0.05 to 0.25
- occupation: float32 [4], replicated, may hold values from 0.1 to 2
- momentum_map: int32 [16, 16], replicated, may hold values from 0 to 15, as said below
Outputs:
- self_energy: bfloat16 [16, 16, 2, 512, 512], P(None, 'energy', None, 'mom')
- density: float32 [512, 16, 2, 512], P('energy', 'mom')
Inputs may be any that keep to these rules, and one draw needn't show every extreme that they name: `shift_steps`: some entry equals 2. `momentum_map`: every row and every column holds each of the 16 momentum indices once.
All inputs are finite; a program needn't handle non-finite values.
Results may differ from a plain program's by a relative error of at most 0.02.
Values may be sent and summed in bfloat16 or wider, within the bound.
No kernel may reach another device: no remote copies, remote signals or barrier semaphores. Data moves between devices by JAX's collectives and lax.ppermute only.
A program may use at most 192 MiB of HBM per device.

v0:
```python
import math

import jax
import jax.numpy as jnp
from jax import lax
from jax.sharding import PartitionSpec as P

SHIFT_MAX = 2


def with_halo(cells, sides, width):
    for axis, dim in sides:
        count = lax.axis_size(axis)
        ends = count - 1
        head = lax.slice_in_dim(cells, 0, width, axis=dim)
        tail = lax.slice_in_dim(cells, cells.shape[dim] - width, cells.shape[dim], axis=dim)
        cells = jnp.concatenate(
            [
                lax.ppermute(tail, axis, [(i, (i + 1) % count) for i in range(ends)]),
                cells,
                lax.ppermute(head, axis, [((i + 1) % count, i) for i in range(ends)]),
            ],
            axis=dim,
        )
    return cells


def scale_columns(green, gamma):
    return (green.astype(jnp.float32) * gamma[:, :, None, None, :]).astype(jnp.bfloat16)


def outer_pair(left, right):
    real_part = jnp.einsum("kecij,kecmj->keim", left, right, preferred_element_type=jnp.float32)
    imag_part = jnp.einsum(
        "keij,kemj->keim", left[:, :, 1], right[:, :, 0], preferred_element_type=jnp.float32
    ) - jnp.einsum(
        "keij,kemj->keim", left[:, :, 0], right[:, :, 1], preferred_element_type=jnp.float32
    )
    return jnp.stack([real_part, imag_part], axis=2)


def complex_product(left, right):
    real_part = jnp.einsum(
        "keij,kejm->keim", left[:, :, 0], right[:, :, 0], preferred_element_type=jnp.float32
    ) - jnp.einsum(
        "keij,kejm->keim", left[:, :, 1], right[:, :, 1], preferred_element_type=jnp.float32
    )
    imag_part = jnp.einsum(
        "keij,kejm->keim", left[:, :, 0], right[:, :, 1], preferred_element_type=jnp.float32
    ) + jnp.einsum(
        "keij,kejm->keim", left[:, :, 1], right[:, :, 0], preferred_element_type=jnp.float32
    )
    return jnp.stack([real_part, imag_part], axis=2)


def shifted_sum(padded, shift_steps, mode_weight, occupation):
    count_energy = padded.shape[1] - 2 * SHIFT_MAX
    total = jnp.zeros((padded.shape[0], count_energy) + padded.shape[2:], jnp.float32)
    for branch in range(shift_steps.shape[0]):
        offset = shift_steps[branch]
        above = lax.dynamic_slice_in_dim(padded, SHIFT_MAX + offset, count_energy, 1).astype(
            jnp.float32
        )
        below = lax.dynamic_slice_in_dim(padded, SHIFT_MAX - offset, count_energy, 1).astype(
            jnp.float32
        )
        total = total + mode_weight[branch] * (
            (occupation[branch] + 1.0) * above + occupation[branch] * below
        )
    return total.astype(jnp.bfloat16)


def convolve_blocks(make_block, coupling, momentum_map, shape):
    rows_tile = shape[3]
    block_rows = math.gcd(16, rows_tile)
    block_count = rows_tile // block_rows

    def one_block(position, result):
        start = position * block_rows
        source = make_block(start, block_rows)
        weights = lax.dynamic_slice_in_dim(coupling, start, block_rows, 1).astype(jnp.float32)
        total = jnp.zeros(source.shape, jnp.float32)
        for qpoint in range(source.shape[0]):
            donor = jnp.take(source, momentum_map[:, qpoint], axis=0).astype(jnp.float32)
            total = total + weights[qpoint][None, None, None] * donor
        return lax.dynamic_update_slice_in_dim(result, total.astype(jnp.bfloat16), start, 3)

    return lax.fori_loop(0, block_count, one_block, jnp.zeros(shape, jnp.bfloat16))


def on_device(green_ret, broadening, coupling, shift_steps, mode_weight, occupation, momentum_map):
    scaled = scale_columns(green_ret, broadening)
    lesser = outer_pair(scaled, green_ret).astype(jnp.bfloat16)
    local_k = green_ret.shape[0]
    norb = green_ret.shape[-1]
    all_k = local_k * lax.axis_size("mom")
    tile_shape = (all_k, green_ret.shape[1], 2, norb // lax.axis_size("mom"), norb)
    padded = with_halo(lesser, (("energy", 1),), SHIFT_MAX)
    source = shifted_sum(padded, shift_steps, mode_weight, occupation)
    tiles = lax.all_to_all(source, "mom", split_axis=3, concat_axis=0, tiled=True)

    def make_block(start, count):
        return lax.dynamic_slice_in_dim(tiles, start, count, 3)

    self_energy = convolve_blocks(make_block, coupling, momentum_map, tile_shape)
    home = lax.all_to_all(self_energy, "mom", split_axis=0, concat_axis=3, tiled=True)
    total_energies = green_ret.shape[1] * lax.axis_size("energy")
    mixed = (complex_product(green_ret, home) + scaled.astype(jnp.float32)).astype(jnp.bfloat16)
    real_part = jnp.einsum("kecij,kecmj->ikm", mixed, green_ret, preferred_element_type=jnp.float32)
    imag_part = jnp.einsum(
        "keij,kemj->ikm", mixed[:, :, 1], green_ret[:, :, 0], preferred_element_type=jnp.float32
    ) - jnp.einsum(
        "keij,kemj->ikm", mixed[:, :, 0], green_ret[:, :, 1], preferred_element_type=jnp.float32
    )
    density = lax.psum_scatter(
        (jnp.stack([real_part, imag_part], axis=2) / total_energies).astype(jnp.bfloat16),
        "energy",
        scatter_dimension=0,
        tiled=True,
    ).astype(jnp.float32)
    return (self_energy, density)


def solution(mesh):
    return jax.shard_map(
        on_device,
        mesh=mesh,
        in_specs=(
            P("mom", "energy", None, None, None),
            P("mom", "energy", None),
            P(None, "mom", None),
            P(),
            P(),
            P(),
            P(),
        ),
        out_specs=(P(None, "energy", None, "mom", None), P("energy", "mom", None, None)),
        check_vma=False,
    )
```

profile of v0, /device:TPU:0, one launch (start us, length us, event | category | flops | bytes accessed | tf_op | source)
XLA Modules:
  0.0 1186.6 jit_solution(6584746059742068872)
XLA Ops:
  7.2 8.7 multiply_convert_fusion
  15.9 9.8 fusion.3
  25.6 7.9 fusion.10
  33.5 7.6 fusion.6
  41.1 2.6 copy.89
  43.8 7.9 pad_maximum_fusion.1
  51.6 8.1 collective-permute-start
  59.8 1.8 collective-permute-start.1
  76.1 340.2 %collective-permute-done = bf16[4,2,2,512,512]{4,3,1,0,2:T(8,128)(2,1)} collective-permute-done((bf16[4,2,2,512,512]{4,3,1,0,2:T(8,128)(2,1)}, bf16[4,2,2,512,512]{4,3,1,0,2:T(8,128)(2,1)}, u32[]{:S(2)}, u32[]{:S(2)}) %collective-permute-start) | collective-permute-done | bytes 8388640 | tf_op jit(solution)/shard_map/ppermute | solution.py:19
  416.3 17.5 %pad_maximum_fusion = bf16[4,6,2,512,512]{4,3,1,0,2:T(8,128)(2,1)} fusion(bf16[4,2,2,512,512]{4,3,1,0,2:T(8,128)(2,1)} %collective-permute-done.1, bf16[4,2,1,512,512]{4,3,1,0,2:T(8,128)(2,1)} %fusion.6, bf16[4,2,1,512,512]{4,3,1,0,2:T(8,128)(2,1)} %bitcast.202, bf16[4,2,2,512,512]{4,3,1,0,2:T(8,128)(2,1)} %collective-permute-done), kind=kLoop, calls=%fused_computation.84 | loop fusion | flops 37748736 | bytes 50331648 | tf_op jit(solution)/shard_map/concatenate | solution.py:17
  433.8 30.5 %add_convert_fusion.1 = bf16[4,2,2,512,512]{4,3,1,0,2:T(8,128)(2,1)S(1)} fusion(bf16[4,6,2,512,512]{4,3,1,0,2:T(8,128)(2,1)} %pad_maximum_fusion, s32[]{:T(128)S(6)} %select_n.47, f32[]{:T(128)} %bitcast.58, s32[]{:T(128)S(6)} %select_n.46, f32[]{:T(128)S(6)} %add.283, f32[]{:T(128)} %bitcast.57, s32[]{:T(128)S(6)} %select_n.45, f32[]{:T(128)} %bitcast.52, ...), kind=kLoop, calls=%fused_computation.87 | loop fusion | flops 117440512 | bytes 75497552 | tf_op jit(solution)/shard_map/convert_element_type | solution.py:70
  464.3 22.3 %copy.27 = bf16[4,2,2,512,512]{4,1,0,2,3:T(2,128)(2,1)} copy(bf16[4,2,2,512,512]{4,3,1,0,2:T(8,128)(2,1)S(1)} %add_convert_fusion.1) | data formatting | bytes 16777216 | tf_op jit(solution)/shard_map/convert_element_type | solution.py:70
  486.7 5.8 all-to-all-start
  492.8 92.8 %all-to-all-done = bf16[4,2,2,512,512]{4,1,0,2,3:T(2,128)(2,1)} async-done(((bf16[4,2,2,512,512]{4,1,0,2,3:T(2,128)(2,1)}), bf16[4,2,2,512,512]{4,1,0,2,3:T(2,128)(2,1)}, u32[]{:S(2)}, u32[]{:S(2)}) %all-to-all-start) | async-done | bytes 8388640 | tf_op jit(solution)/shard_map/all_to_all | solution.py:100
  585.6 11.5 copy.28
  597.1 4.4 broadcast_in_dim.13
  601.5 285.4 %while.13 = (s32[]{:T(128)}, bf16[16,2,2,128,512]{4,3,2,1,0:T(8,128)(2,1)}, bf16[16,128,512]{2,1,0:T(8,128)(2,1)}, bf16[16,2,2,128,512]{4,3,2,1,0:T(8,128)(2,1)}...) while((s32[]{:T(128)}, bf16[16,2,2,128,512]{4,3,2,1,0:T(8,128)(2,1)}, ...), condition=%wide.region_1.3_spmd, body=%wide.region_0.2_spmd.sunk | while | flops 33703428 | bytes 55906968 | solution.py:88
  623.4 1.6 gather_fusion.15
  627.6 9.5 fusion.31
  659.0 1.6 gather_fusion.15
  663.3 9.5 fusion.31
  694.7 1.6 gather_fusion.15
  699.0 9.5 fusion.31
  730.4 1.6 gather_fusion.15
  734.7 9.5 fusion.31
  766.1 1.6 gather_fusion.15
  770.3 9.5 fusion.31
  801.7 1.6 gather_fusion.15
  806.0 9.5 fusion.31
  837.4 1.6 gather_fusion.15
  841.7 9.5 fusion.31
  873.1 1.6 gather_fusion.15
  877.4 9.5 fusion.31
  886.9 100.8 %all_to_all.36 = bf16[16,2,2,128,512]{4,3,2,1,0:T(8,128)(2,1)} all-to-all(bf16[16,2,2,128,512]{4,3,2,1,0:T(8,128)(2,1)} %get-tuple-element.110), channel_id=1, replica_groups=mesh['energy'=8,'mom'=4] {'mom'}, dimensions={0} | all-to-all | bytes 16777216 | tf_op jit(solution)/shard_map/all_to_all | solution.py:106
  987.7 13.7 %copy.30 = bf16[4,4,2,2,128,512]{4,0,5,2,1,3:T(4,128)(2,1)} copy(bf16[4,4,2,2,128,512]{5,4,3,2,1,0:T(8,128)(2,1)} %bitcast.204) | data formatting | bytes 16777216 | tf_op jit(solution)/shard_map/all_to_all | solution.py:106
  1001.4 13.1 %all_to_all.33 = bf16[4,2,2,512,512]{3,4,1,0,2:T(8,128)(2,1)} reshape(bf16[4,2,2,4,128,512]{4,3,5,1,0,2:T(4,128)(2,1)} %bitcast.203) | data formatting | bytes 16777216 | tf_op jit(solution)/shard_map/all_to_all | solution.py:106
  1014.5 9.2 fusion.14
  1023.7 8.0 fusion.13
  1031.7 10.4 subtract_bitcast_fusion
  1042.1 10.4 add_bitcast_fusion
  1052.6 7.7 fusion.1
  1060.3 3.3 copy-done.2
  1063.5 4.4 fusion.8
  1067.9 9.7 convolution_bitcast_fusion
  1077.6 7.0 fusion.12
  1084.6 2.6 fusion.2
  1087.3 89.7 %reduce-scatter.2.cloned.1.call-done = bf16[64,4,2,512]{3,0,1,2:T(8,128)(2,1)} async-done(((bf16[512,4,2,512]{3,0,1,2:T(8,128)(2,1)}), bf16[64,4,2,512]{3,0,1,2:T(8,128)(2,1)}) %reduce-scatter.2.cloned.1.call-update) | async-done | bytes 524304 | tf_op jit(solution)/shard_map/reduce_scatter | solution.py:115
  1177.0 2.6 copy.37
  (250 shorter events, 197.8 us)
Async XLA Ops:
  7.2 8.7 copy-start.3
  7.2 18.5 %slice-start = ((s8[8388608]{0:T(1024)(128)(4,1)}), s8[4194304]{0:T(1024)(128)(4,1)S(1)}, s32[]{:S(2)}) async-start(s8[8388608]{0:T(1024)(128)(4,1)} %bitcast.197), calls=%async_computation.4 | async-start | bytes 8388608
  15.9 9.8 slice-start.1
  43.7 7.9 copy-start.1
  43.7 17.9 %copy-start.6 = (s32[4]{0:T(128)S(1)}, s32[4]{0:T(128)}, u32[]{:S(2)}) copy-start(s32[4]{0:T(128)} %param.14) | copy-start | bytes 52
  43.7 28.4 %copy-start.7 = (f32[4]{0:T(128)S(1)}, f32[4]{0:T(128)}, u32[]{:S(2)}) copy-start(f32[4]{0:T(128)} %param.16) | copy-start | bytes 52
  43.7 31.7 %copy-start.8 = (f32[4]{0:T(128)S(1)}, f32[4]{0:T(128)}, u32[]{:S(2)}) copy-start(f32[4]{0:T(128)} %param.15) | copy-start | bytes 52
  51.6 364.7 %collective-permute-start = (bf16[4,2,2,512,512]{4,3,1,0,2:T(8,128)(2,1)}, bf16[4,2,2,512,512]{4,3,1,0,2:T(8,128)(2,1)}, u32[]{:S(2)}, u32[]{:S(2)}) collective-permute-start(bf16[4,2,2,512,512]{4,3,1,0,2:T(8,128)(2,1)} %pad_maximum_fusion.1), channel_id=1, source_target_pairs={{0,4},{4,8},{8,12},{12,16},{16,20},{20,24},{24,28},{1,5},{5,9},{9,... | collective-permute-start | bytes 25165832 | tf_op jit(solution)/shard_map/ppermute | solution.py:19
  59.8 356.5 %collective-permute-start.1 = (bf16[4,2,2,512,512]{4,3,1,0,2:T(8,128)(2,1)}, bf16[4,2,2,512,512]{4,3,1,0,2:T(8,128)(2,1)}, u32[]{:S(2)}, u32[]{:S(2)}) collective-permute-start(bf16[4,2,2,512,512]{4,3,1,0,2:T(8,128)(2,1)} %pad_maximum_fusion.1), channel_id=1, source_target_pairs={{4,0},{8,4},{12,8},{16,12},{20,16},{24,20},{28,24},{5,1},{9,5},{13... | collective-permute-start | bytes 25165832 | tf_op jit(solution)/shard_map/ppermute | solution.py:21
  486.7 6.0 copy-start.5
  486.7 98.9 %all-to-all-start = ((bf16[4,2,2,512,512]{4,1,0,2,3:T(2,128)(2,1)}), bf16[4,2,2,512,512]{4,1,0,2,3:T(2,128)(2,1)}, u32[]{:S(2)}, u32[]{:S(2)}) async-start(bf16[4,2,2,512,512]{4,1,0,2,3:T(2,128)(2,1)} %copy.27), calls=%async_computation | async-start | bytes 16777216 | tf_op jit(solution)/shard_map/all_to_all | solution.py:100
  492.5 684.5 %reduce-scatter.2.cloned.1.call-start = ((), (), s32[]{:S(2)}) async-start(), calls=%async_computation.3 | async-start | bytes 4718592 | tf_op jit(solution)/shard_map/reduce_scatter | solution.py:115
  1014.5 9.2 copy-start
  1014.5 17.2 %slice-start.2 = ((s8[8388608]{0:T(1024)(128)(4,1)}), s8[4194304]{0:T(1024)(128)(4,1)S(1)}, s32[]{:S(2)}) async-start(s8[8388608]{0:T(1024)(128)(4,1)} %bitcast.199), calls=%async_computation.6 | async-start | bytes 8388608
  1023.7 8.0 slice-start.3
  1042.1 10.4 copy-start.4
  1060.3 3.3 copy-start.2
Sparse Core Ops, SparseCore 0:
  1087.4 89.5 reduce-scatter.1
where the time goes:
time: 1190 us
  waiting for transfers between devices  523 us (44%)
  local copies, waits for them, and re-layouts  275 us (23%)
  other arithmetic  160 us (13%)
  blocking collectives  101 us (8%)
  matrix products  84.3 us (7%)
  between operations  27 us (2%)
  starting transfers between devices  16 us (1%)
    ppermute x1, waiting for transfers between devices, with_halo(): lax.ppermute(tail, axis, [(i, (i + 1) % count) for i in range(ends)])  340 us
    gather x128, local copies, waits for them, and re-layouts, one_block(): jnp.take(source, momentum_map[:, qpoint], axis=0).astype(jnp.float32)  189 us
    all_to_all x1, blocking collectives, on_device(): lax.all_to_all(self_energy, 'mom', split_axis=0, concat_axis=3, tiled=True)  101 us
    all_to_all x1, waiting for transfers between devices, on_device(): lax.all_to_all(source, 'mom', split_axis=3, concat_axis=0, tiled=True)  92.8 us
    reduce_scatter x1, waiting for transfers between devices, on_device(): lax.psum_scatter((jnp.stack([real_part, imag_part], axis=2) / total_energ...  89.7 us
    dynamic_update_slice x8, other arithmetic, one_block(): lax.dynamic_update_slice_in_dim(result, total.astype(jnp.bfloat16), start...  76 us
    convert_element_type x1, other arithmetic, shifted_sum(): return total.astype(jnp.bfloat16)  30.5 us
    all_to_all x2, local copies, waits for them, and re-layouts, on_device(): lax.all_to_all(self_energy, 'mom', split_axis=0, concat_axis=3, tiled=True)  26.8 us
  transfers between devices with their start and end apart: 4, of which 3 were waited for; matrix products, arithmetic and copies ran while one was open for 0% of the time, Pallas kernels for 0%

commit v1 on v0

v1 whole, which is shorter than its diff:
```python
import functools

import jax
import jax.numpy as jnp
from jax import lax
from jax.experimental import pallas as pl
from jax.experimental.pallas import tpu as pltpu
from jax.sharding import PartitionSpec as P

SHIFT_MAX = 2
F32 = jnp.float32
BF16 = jnp.bfloat16


def params(**kw):
    return pltpu.CompilerParams(vmem_limit_bytes=56 * 1024 * 1024, **kw)


def cost(flops, nbytes):
    return pl.CostEstimate(flops=int(flops), bytes_accessed=int(nbytes), transcendentals=0)


def dot_nt(a, b):
    return lax.dot_general(a, b, (((1,), (1,)), ((), ())), preferred_element_type=F32)


def dot_nn(a, b):
    return lax.dot_general(a, b, (((1,), (0,)), ((), ())), preferred_element_type=F32)


def row_col(rows, cols):
    return lax.broadcasted_iota(jnp.int32, (rows, cols), 0), lax.broadcasted_iota(jnp.int32, (rows, cols), 1)


def lesser_kernel(sel, g_ref, gamma_ref, out_ref):
    n = g_ref.shape[-1]
    half = n // 2
    e = pl.program_id(1)
    gamma = gamma_ref[0, pl.ds(e, 1), :]
    g_re, g_im = g_ref[0, 0, 0], g_ref[0, 0, 1]
    s_re = (g_re.astype(F32) * gamma).astype(BF16)
    s_im = (g_im.astype(F32) * gamma).astype(BF16)
    row, col = row_col(half, half)

    def real(i, j):
        i, j = slice(i * half, (i + 1) * half), slice(j * half, (j + 1) * half)
        return dot_nt(s_re[i], g_re[j]) + dot_nt(s_im[i], g_im[j])

    def imag(i, j):
        i, j = slice(i * half, (i + 1) * half), slice(j * half, (j + 1) * half)
        return dot_nt(s_im[i], g_re[j]) - dot_nt(s_re[i], g_im[j])

    for d in range(2):
        out_ref[0, 0, d * half:(d + 1) * half, d * half:(d + 1) * half] = jnp.where(
            col >= row, real(d, d), imag(d, d)).astype(BF16)
    out_ref[0, 0, :half, half:] = real(0, 1).astype(BF16)
    out_ref[0, 0, half:, :half] = imag(1, 0).astype(BF16)


def lesser_packed(block, green, broadening, count):
    _, le, _, n, _ = green.shape
    return pl.pallas_call(
        lesser_kernel,
        out_shape=jax.ShapeDtypeStruct((count, le, n, n), BF16),
        grid_spec=pltpu.PrefetchScalarGridSpec(
            num_scalar_prefetch=1,
            grid=(count, le),
            in_specs=[
                pl.BlockSpec((1, 1, 2, n, n), lambda k, e, sel: (sel[0] * count + k, e, 0, 0, 0)),
                pl.BlockSpec((1, le, n), lambda k, e, sel: (sel[0] * count + k, 0, 0)),
            ],
            out_specs=pl.BlockSpec((1, 1, n, n), lambda k, e, sel: (k, e, 0, 0)),
        ),
        compiler_params=params(),
        cost_estimate=cost(count * le * 6 * n**3, count * le * n * n * 6),
        name="lesser",
    )(block, green, broadening)


def source_kernel(odd, w_ref, keep, recv, kz, rz, *outs):
    le = keep.shape[1]

    def emit(order):
        line = [(ref, e) for ref in order for e in range(le)]
        for e in range(le):
            for ref, target in ((keep, outs[e]), (recv, outs[le + e])):
                at = [i for i, held in enumerate(order) if held is ref][0] * le + e
                total = None
                for s in range(1, SHIFT_MAX + 1):
                    for j, sign in ((0, s), (1, -s)):
                        source, index = line[at + sign]
                        term = w_ref[2 * (s - 1) + j] * source[0, index].astype(F32)
                        total = term if total is None else total + term
                target[0] = total.astype(BF16)

    @pl.when(odd[0] == 0)
    def _():
        emit((rz, keep, recv, kz))

    @pl.when(odd[0] == 1)
    def _():
        emit((kz, recv, keep, rz))


def sources(odd, weights, keep, recv, kz, rz):
    count, le, n, _ = keep.shape
    rows = n // 4
    big = pl.BlockSpec((1, le, rows, n), lambda k, r, *_: (k, 0, r, 0))
    one = pl.BlockSpec((1, rows, n), lambda k, r, *_: (k, r, 0))
    return pl.pallas_call(
        source_kernel,
        out_shape=[jax.ShapeDtypeStruct((count, n, n), BF16)] * (2 * le),
        grid_spec=pltpu.PrefetchScalarGridSpec(
            num_scalar_prefetch=2,
            grid=(count, n // rows),
            in_specs=[big] * 4,
            out_specs=[one] * (2 * le),
        ),
        compiler_params=params(),
        cost_estimate=cost(count * le * n * n * 16, count * le * n * n * 12),
        name="source",
    )(odd, weights, keep, recv, kz, rz)


def home_kernel(lk, pieces, slots, *refs):
    ins, (c_ref, ct_ref, x_ref, y_ref, q_ref) = refs[:pieces], refs[pieces:]
    each, rows, n = ins[0].shape
    for s in range(pieces):
        for j in range(each):
            q_ref[s * each + j] = ins[s][j].astype(F32)
    count = pieces * each
    tr, tc = 16, 256

    def tile(index, _):
        r = pl.ds(pl.multiple_of((index // (n // tc)) * tr, tr), tr)
        m = pl.ds(pl.multiple_of((index % (n // tc)) * tc, tc), tc)
        xs, ys = [None] * lk, [None] * lk
        for q in range(count):
            c, ct = c_ref[0, q, r, m].astype(F32), ct_ref[q, r, m].astype(F32)
            for k in range(lk):
                v = q_ref[slots[k * count + q], r, m]
                xs[k] = c * v if q == 0 else xs[k] + c * v
                ys[k] = ct * v if q == 0 else ys[k] + ct * v
        for k in range(lk):
            x_ref[k, r, m] = xs[k].astype(BF16)
            y_ref[k, r, m] = ys[k].astype(BF16)
        return 0

    lax.fori_loop(0, (rows // tr) * (n // tc), tile, 0)


def home_blocks(slots, pieces, c4, ct, lk):
    each, n, _ = pieces[0].shape
    count = each * len(pieces)
    rows = 64
    per = c4.shape[2] // rows
    return pl.pallas_call(
        functools.partial(home_kernel, lk, len(pieces)),
        out_shape=[jax.ShapeDtypeStruct((lk, n, n), BF16)] * 2,
        grid_spec=pltpu.PrefetchScalarGridSpec(
            num_scalar_prefetch=1,
            grid=(n // rows,),
            in_specs=[pl.BlockSpec((each, rows, n), lambda g, s: (0, g, 0))] * len(pieces) + [
                pl.BlockSpec((1, count, rows, n), lambda g, s: (g // per, 0, g % per, 0)),
                pl.BlockSpec((count, rows, n), lambda g, s: (0, g, 0)),
            ],
            out_specs=[pl.BlockSpec((lk, rows, n), lambda g, s: (0, g, 0))] * 2,
            scratch_shapes=[pltpu.VMEM((count, rows, n), F32)],
        ),
        compiler_params=params(),
        cost_estimate=cost(4 * lk * count * n * n, n * n * (6 * count + 4 * lk)),
        name="home",
    )(slots, *pieces, c4, ct)


def rows_kernel(pieces, aliased, mine, slots, *refs):
    a_refs, b_refs, refs = refs[:pieces], refs[pieces:2 * pieces], refs[2 * pieces:]
    c_ref, out_ref, re_ref, im_ref = (refs[0],) + refs[-3:]
    each, rows, cols = a_refs[0].shape
    count = pieces * each
    row, col = row_col(rows, cols)
    above = (col - row) + (pl.program_id(0) * cols - mine[0] * rows)
    for s in range(pieces):
        for j in range(each):
            a, b = a_refs[s][j].astype(F32), b_refs[s][j].astype(F32).T
            re_ref[s * each + j] = jnp.where(above >= 0, a, b)
            im_ref[s * each + j] = jnp.where(above < 0, a, jnp.where(above > 0, -b, 0.0))
    tr, kg = 16, 8

    def tile(index, _):
        r = pl.ds(pl.multiple_of((index % (rows // tr)) * tr, tr), tr)
        k0 = (index // (rows // tr)) * kg
        res, ims = [None] * kg, [None] * kg
        for q in range(count):
            c = c_ref[q, r, :].astype(F32)
            for k in range(kg):
                slot = slots[(k0 + k) * count + q]
                u, v = c * re_ref[slot, r, :], c * im_ref[slot, r, :]
                res[k] = u if q == 0 else res[k] + u
                ims[k] = v if q == 0 else ims[k] + v
        for k in range(kg):
            out_ref[k0 + k, 0, 0, r, :] = res[k].astype(BF16)
            out_ref[k0 + k, 0, 1, r, :] = ims[k].astype(BF16)
        return 0

    lax.fori_loop(0, (rows // tr) * (count // kg), tile, 0)


def own_rows(mine, slots, pieces, coupling, energy, le, held):
    each, n, _ = pieces[0].shape
    count, rows, _ = coupling.shape
    cols = rows
    alias = held is not None
    out_map = lambda t, mine, slots: (0, energy, 0, 0, t)
    in_specs = (
        [pl.BlockSpec((each, rows, cols), lambda t, mine, slots: (0, mine[0], t))] * len(pieces)
        + [pl.BlockSpec((each, cols, rows), lambda t, mine, slots: (0, t, mine[0]))] * len(pieces)
        + [pl.BlockSpec((count, rows, cols), lambda t, mine, slots: (0, 0, t))]
        + ([pl.BlockSpec(memory_space=pl.ANY)] if alias else [])
    )
    return pl.pallas_call(
        functools.partial(rows_kernel, len(pieces), alias),
        out_shape=jax.ShapeDtypeStruct((count, le, 2, rows, n), BF16),
        grid_spec=pltpu.PrefetchScalarGridSpec(
            num_scalar_prefetch=2,
            grid=(n // cols,),
            in_specs=in_specs,
            out_specs=pl.BlockSpec((count, 1, 2, rows, cols), out_map),
            scratch_shapes=[pltpu.VMEM((count, rows, cols), F32)] * 2,
        ),
        input_output_aliases={2 + len(in_specs) - 1: 0} if alias else {},
        compiler_params=params(),
        cost_estimate=cost(4 * count * count * rows * n, rows * n * count * 10),
        name="rows",
    )(mine, slots, *pieces, *pieces, coupling, *([held] if alias else []))


def density_kernel(scale, energy, first, last, g_ref, gamma_ref, x_ref, y_ref, *refs):
    out_ref = refs[-1]
    n = g_ref.shape[-1]
    gamma = gamma_ref[0, energy:energy + 1, :]
    g_re, g_im = g_ref[0, 0, 0], g_ref[0, 0, 1]
    row, col = row_col(n, n)
    x, yt = x_ref[0].astype(F32), y_ref[0].astype(F32).T
    s_re = jnp.where(col >= row, x, yt).astype(BF16)
    s_im = jnp.where(col < row, x, jnp.where(col > row, -yt, 0.0)).astype(BF16)
    scaled_re = (g_re.astype(F32) * gamma).astype(BF16).astype(F32)
    scaled_im = (g_im.astype(F32) * gamma).astype(BF16).astype(F32)
    m_re = (dot_nn(g_re, s_re) - dot_nn(g_im, s_im) + scaled_re).astype(BF16)
    m_im = (dot_nn(g_re, s_im) + dot_nn(g_im, s_re) + scaled_im).astype(BF16)
    d_re = dot_nt(m_re, g_re) + dot_nt(m_im, g_im)
    d_im = dot_nt(m_im, g_re) - dot_nt(m_re, g_im)
    if not first:
        d_re, d_im = d_re + refs[0][0, 0], d_im + refs[0][0, 1]
    if last:
        d_re, d_im = d_re * scale, d_im * scale
    out_ref[0, 0] = d_re.astype(out_ref.dtype)
    out_ref[0, 1] = d_im.astype(out_ref.dtype)


def density_term(scale, energy, le, green, broadening, x, y, held):
    lk, _, _, n, _ = green.shape
    last = energy == le - 1
    pair = pl.BlockSpec((1, 2, n, n), lambda k: (k, 0, 0, 0))
    one = pl.BlockSpec((1, n, n), lambda k: (k, 0, 0))
    return pl.pallas_call(
        functools.partial(density_kernel, scale, energy, held is None, last),
        out_shape=jax.ShapeDtypeStruct((lk, 2, n, n), BF16 if last else F32),
        grid=(lk,),
        in_specs=[
            pl.BlockSpec((1, 1, 2, n, n), lambda k: (k, energy, 0, 0, 0)),
            pl.BlockSpec((1, le, n), lambda k: (k, 0, 0)),
            one,
            one,
        ] + ([] if held is None else [pair]),
        out_specs=pair,
        compiler_params=params(),
        cost_estimate=cost(16 * lk * n**3, lk * n * n * 20),
        name="density",
    )(green, broadening, x, y, *([] if held is None else [held]))


def on_device(green_ret, broadening, coupling, shift_steps, mode_weight, occupation, momentum_map):
    lk, le, _, n, _ = green_ret.shape
    ne, nm = lax.axis_size("energy"), lax.axis_size("mom")
    if le != SHIFT_MAX or lk % 2 or ne % 2 or nm & (nm - 1):
        raise ValueError("unsupported sizes")
    hk, nk = lk // 2, lk * nm
    me, mine = lax.axis_index("energy"), lax.axis_index("mom")
    odd = (me % 2).astype(jnp.int32)
    pairs = [(i, i ^ 1) for i in range(ne)]
    away = [(i, i + (2 if i % 2 else -2)) for i in range(ne) if 0 <= i + (2 if i % 2 else -2) < ne]
    across = [(i, i + (-2 if i % 2 else 2)) for i in range(ne) if 0 <= i + (-2 if i % 2 else 2) < ne]

    def swap(x, stride):
        return lax.ppermute(x, "mom", [(i, i ^ stride) for i in range(nm)])

    c4 = lax.all_gather(coupling, "mom", axis=0)
    ct = jnp.transpose(c4, (1, 3, 0, 2)).reshape(nk, n, n)

    weights = []
    for s in range(1, SHIFT_MAX + 1):
        held = shift_steps == s
        weights.append(jnp.sum(jnp.where(held, mode_weight * (occupation + 1.0), 0.0)))
        weights.append(jnp.sum(jnp.where(held, mode_weight * occupation, 0.0)))
    weights = jnp.stack(weights)

    send = lesser_packed((1 - odd)[None], green_ret, broadening, hk)
    recv = lax.ppermute(send, "energy", pairs)
    keep = lesser_packed(odd[None], green_ret, broadening, hk)
    kz = lax.ppermute(keep, "energy", away)
    rz = lax.ppermute(recv, "energy", across)
    got = sources(odd[None], weights, keep, recv, kz, rz)

    owner, inner = momentum_map // lk, momentum_map % lk
    relative = owner ^ mine
    strides = []
    stride = nm // 2
    while stride:
        strides.append(stride)
        stride //= 2
    place = jnp.zeros_like(relative)
    for bit, s in enumerate(strides):
        place = place + jnp.where((relative & s) != 0, 1 << bit, 0)
    slots = (place * lk + ((inner // hk) ^ odd) * hk + inner % hk).astype(jnp.int32)
    own_slots = lax.dynamic_slice_in_dim(slots, mine * lk, lk, 0).reshape(-1)
    all_slots = slots.reshape(-1)
    mine_ref = mine.astype(jnp.int32)[None]

    held_rows, held_density = None, None
    scale = 1.0 / (le * ne)
    for e in range(le):
        back = lax.ppermute(got[le + e], "energy", pairs)
        pieces = [got[e], back]
        for s in strides:
            pieces = pieces + [swap(piece, s) for piece in pieces]
        x, y = home_blocks(own_slots, pieces, c4, ct, lk)
        held_density = density_term(scale, e, le, green_ret, broadening, x, y, held_density)
        held_rows = own_rows(mine_ref, all_slots, pieces, coupling, e, le, held_rows)
    density = lax.psum_scatter(held_density, "energy", scatter_dimension=2, tiled=True)
    return held_rows, jnp.transpose(density, (2, 0, 1, 3)).astype(F32)


def solution(mesh):
    return jax.shard_map(
        on_device,
        mesh=mesh,
        in_specs=(
            P("mom", "energy", None, None, None),
            P("mom", "energy", None),
            P(None, "mom", None),
            P(),
            P(),
            P(),
            P(),
        ),
        out_specs=(P(None, "energy", None, "mom", None), P("energy", "mom", None, None)),
        check_vma=False,
    )
```

time: 1190 us -> 411 us (0.35)
  waiting for transfers between devices: 523 us -> 211 us
  local copies, waits for them, and re-layouts: 275 us -> 31.2 us
  other arithmetic: 160 us -> 5.02 us
  Pallas kernels: 0 us -> 131 us
  blocking collectives: 101 us -> 0 us
  matrix products: 84.3 us -> 0 us
  between operations: 27 us -> 14.2 us
    gather x128 -> x0, local copies, waits for them, and re-layouts: 189 us -> none  [one_block(): jnp.take(source, momentum_map[:, qpoint], axis=0).astype(jnp.float32)]
    ppermute x2 -> x17, waiting for transfers between devices: 340 us -> 162 us  [the longest x12 44.5 us: swap(): return lax.ppermute(x, 'mom', [(i, i ^ stride) for i in range(nm)])]
    pallas_call x0 -> x9, Pallas kernels: none -> 131 us  [the longest x2 41.7 us: home_blocks(): pl.pallas_call(functools.partial(home_kernel, lk, len(pieces)), out_shape...]
    all_to_all x1 -> x0, blocking collectives: 101 us -> none  [on_device(): lax.all_to_all(self_energy, 'mom', split_axis=0, concat_axis=3, tiled=True)]
    all_to_all x1 -> x0, waiting for transfers between devices: 92.8 us -> none  [on_device(): lax.all_to_all(source, 'mom', split_axis=3, concat_axis=0, tiled=True)]
    dot_general x10 -> x0, matrix products: 84.3 us -> none  [the longest x1 10.4 us: complex_product(): jnp.einsum('keij,kejm->keim', left[:, :, 1], right[:, :, 1], preferred_el...]
    dynamic_update_slice x8 -> x0, other arithmetic: 76 us -> none  [one_block(): lax.dynamic_update_slice_in_dim(result, total.astype(jnp.bfloat16), start...]
    convert_element_type x12 -> x1, other arithmetic: 57.5 us -> 1.15 us  [on_device(): return (held_rows, jnp.transpose(density, (2, 0, 1, 3)).astype(F32))]
  transfers between devices with their start and end apart: 4 -> 19, of which waited for: 3 -> 9; matrix products, arithmetic and copies ran while one was open for 0% -> 8% of each run, Pallas kernels for 0% -> 24%
where the time goes in v1:
time: 411 us; the launch traced here: 409 us
  waiting for transfers between devices  211 us (51%)
  Pallas kernels  131 us (32%)
  local copies, waits for them, and re-layouts  31.2 us (8%)
  starting transfers between devices  16.9 us (4%)
  between operations  14.2 us (3%)
  other arithmetic  5.02 us (1%)
    reduce_scatter x1, waiting for transfers between devices, on_device(): lax.psum_scatter(held_density, 'energy', scatter_dimension=2, tiled=True)  48.7 us
    ppermute x12, waiting for transfers between devices, swap(): return lax.ppermute(x, 'mom', [(i, i ^ stride) for i in range(nm)])  44.5 us
    pallas_call x2, Pallas kernels, home_blocks(): pl.pallas_call(functools.partial(home_kernel, lk, len(pieces)), out_shape...  41.7 us
    ppermute x2, waiting for transfers between devices, on_device(): back = lax.ppermute(got[le + e], 'energy', pairs)  40.1 us
    pallas_call x2, Pallas kernels, own_rows(): pl.pallas_call(functools.partial(rows_kernel, len(pieces), alias), out_sh...  39.6 us
    ppermute x1, waiting for transfers between devices, on_device(): rz = lax.ppermute(recv, 'energy', across)  37.6 us
    ppermute x1, waiting for transfers between devices, on_device(): recv = lax.ppermute(send, 'energy', pairs)  37.6 us
    pallas_call x2, Pallas kernels, density_term(): pl.pallas_call(functools.partial(density_kernel, scale, energy, held is N...  26.3 us
  transfers between devices with their start and end apart: 19, of which 9 were waited for; matrix products, arithmetic and copies ran while one was open for 8% of the time, Pallas kernels for 24%

profile of v1, /device:TPU:0, one launch (start us, length us, event | category | flops | bytes accessed | tf_op | source)
XLA Modules:
  0.0 409.3 jit_solution(17823506895121476766)
XLA Ops:
  7.2 0.0 all-gather.3.cloned.1.call-start
  7.2 0.7 all-gather.3.cloned.1.call-update
  7.9 0.0 reduce-scatter.2.cloned.1.call-start
  8.0 6.7 %lesser.3 = bf16[2,2,512,512]{3,2,1,0:T(8,128)(2,1)} custom-call(s32[1]{0:T(128)} %bitcast.6.sel, bf16[4,2,2,512,512]{4,3,2,1,0:T(8,128)(2,1)} %g_ref.7, f32[4,2,512]{2,1,0:T(2,128)} %gamma_ref.7), custom_call_target="tpu_custom_call" | custom-call | flops 3221225472 | bytes 6291456 | tf_op jit(solution)/shard_map/lesser/pallas_call | solution.py:62
  14.7 3.0 collective-permute-start
  17.7 7.0 %lesser.2.keep = bf16[2,2,512,512]{3,2,1,0:T(8,128)(2,1)} custom-call(s32[1]{0:T(128)} %bitcast.1.sel.odd, bf16[4,2,2,512,512]{4,3,2,1,0:T(8,128)(2,1)} %g_ref.7, f32[4,2,512]{2,1,0:T(2,128)} %gamma_ref.7), custom_call_target="tpu_custom_call" | custom-call | flops 3221225472 | bytes 6291456 | tf_op jit(solution)/shard_map/lesser/pallas_call | solution.py:62
  24.6 1.3 collective-permute-start.1
  25.9 37.6 %collective-permute-done.recv = bf16[2,2,512,512]{3,2,1,0:T(8,128)(2,1)S(1)} collective-permute-done((bf16[2,2,512,512]{3,2,1,0:T(8,128)(2,1)}, bf16[2,2,512,512]{3,2,1,0:T(8,128)(2,1)S(1)}, u32[]{:S(2)}, u32[]{:S(2)}) %collective-permute-start) | collective-permute-done | bytes 2097184 | tf_op jit(solution)/shard_map/ppermute | solution.py:309
  63.5 4.0 collective-permute-start.2
  67.5 0.7 fusion.11
  68.2 3.1 pad_maximum_fusion.w_ref
  71.4 2.3 collective-permute-done.1.kz
  73.7 37.6 %collective-permute-done.2.rz = bf16[2,2,512,512]{3,2,1,0:T(8,128)(2,1)S(1)} collective-permute-done((bf16[2,2,512,512]{3,2,1,0:T(8,128)(2,1)S(1)}, bf16[2,2,512,512]{3,2,1,0:T(8,128)(2,1)S(1)}, u32[]{:S(2)}, u32[]{:S(2)}) %collective-permute-start.2) | collective-permute-done | bytes 2097184 | tf_op jit(solution)/shard_map/ppermute | solution.py:312
  111.3 1.3 copy-done.6
  112.6 9.3 %source.1 = (bf16[2,512,512]{2,1,0:T(8,128)(2,1)}, bf16[2,512,512]{2,1,0:T(8,128)(2,1)}, bf16[2,512,512]{2,1,0:T(8,128)(2,1)}, bf16[2,512,512]{2,1,0:T(8,128)(2,1)}) custom-call(s32[1]{0:T(128)} %bitcast.1.sel.odd, f32[4]{0:T(128)} %pad_maximum_fusion.w_ref, bf16[2,2,512,512]{3,2,1,0:T(8,128)(2,1)} %lesser.2.keep, bf16[2,2,512,512]{3,2,1,0:T(8,128)(2,1)} %copy-done.4, ...), custom_call_target="tpu_custom_call" | custom-call | flops 16777216 | bytes 12582912 | tf_op jit(solution)/shard_map/source/pallas_call | solution.py:110
  121.9 2.4 collective-permute-start.10
  124.3 1.5 collective-permute-start.11
  125.8 0.0 collective-permute-start.13
  125.8 0.1 collective-permute-start.3
  125.9 22.7 %collective-permute-done.10.refs_1_.refs_9_ = bf16[2,512,512]{2,1,0:T(8,128)(2,1)S(1)} collective-permute-done((bf16[2,512,512]{2,1,0:T(8,128)(2,1)}, bf16[2,512,512]{2,1,0:T(8,128)(2,1)S(1)}, u32[]{:S(2)}, u32[]{:S(2)}) %collective-permute-start.10) | collective-permute-done | bytes 1048608 | tf_op jit(solution)/shard_map/ppermute | solution.py:333
  148.5 1.5 collective-permute-start.12
  150.0 0.5 collective-permute-start.4
  150.6 0.0 collective-permute-done.13.refs_4_.refs_12_
  150.6 0.5 collective-permute-start.15
  151.1 17.5 %collective-permute-done.3.refs_1_.refs_9_ = bf16[2,512,512]{2,1,0:T(8,128)(2,1)S(1)} collective-permute-done((bf16[2,512,512]{2,1,0:T(8,128)(2,1)}, bf16[2,512,512]{2,1,0:T(8,128)(2,1)S(1)}, u32[]{:S(2)}, u32[]{:S(2)}) %collective-permute-start.3) | collective-permute-done | bytes 1048608 | tf_op jit(solution)/shard_map/ppermute | solution.py:333
  168.5 1.5 collective-permute-start.5
  170.0 4.6 %collective-permute-done.12.refs_3_.refs_11_ = bf16[2,512,512]{2,1,0:T(8,128)(2,1)} collective-permute-done((bf16[2,512,512]{2,1,0:T(8,128)(2,1)S(1)}, bf16[2,512,512]{2,1,0:T(8,128)(2,1)}, u32[]{:S(2)}, u32[]{:S(2)}) %collective-permute-start.12) | collective-permute-done | bytes 1048608 | tf_op jit(solution)/shard_map/ppermute | solution.py:296
  174.7 22.5 %collective-permute-done.4.refs_2_.refs_10_ = bf16[2,512,512]{2,1,0:T(8,128)(2,1)} collective-permute-done((bf16[2,512,512]{2,1,0:T(8,128)(2,1)}, bf16[2,512,512]{2,1,0:T(8,128)(2,1)}, u32[]{:S(2)}, u32[]{:S(2)}) %collective-permute-start.4) | collective-permute-done | bytes 1048608 | tf_op jit(solution)/shard_map/ppermute | solution.py:296
  197.1 0.0 collective-permute-done.14.refs_5_.refs_13_
  197.1 0.5 collective-permute-start.7
  197.6 0.0 collective-permute-done.15.refs_6_.refs_14_
  197.6 0.1 collective-permute-start.8
  197.7 17.3 %collective-permute-done.5.refs_3_.refs_11_ = bf16[2,512,512]{2,1,0:T(8,128)(2,1)} collective-permute-done((bf16[2,512,512]{2,1,0:T(8,128)(2,1)S(1)}, bf16[2,512,512]{2,1,0:T(8,128)(2,1)}, u32[]{:S(2)}, u32[]{:S(2)}) %collective-permute-start.5) | collective-permute-done | bytes 1048608 | tf_op jit(solution)/shard_map/ppermute | solution.py:296
  215.0 0.0 collective-permute-start.9
  215.1 0.6 reshape.14.slots
  215.7 13.6 %copy.12 = bf16[16,512,4,128]{3,2,1,0:T(4,128)(2,1)} copy(bf16[16,512,4,128]{1,3,0,2:T(8,128)(2,1)} %bitcast.12) | data formatting | bytes 16777216 | tf_op jit(solution)/shard_map/transpose | solution.py:299
  229.4 13.1 %reshape.15.refs_9_ = bf16[16,512,512]{2,1,0:T(8,128)(2,1)} reshape(bf16[16,512,4,128]{3,2,1,0:T(4,128)(2,1)} %copy.12) | data formatting | bytes 16777216 | tf_op jit(solution)/shard_map/reshape | solution.py:299
  242.5 20.9 %home.3 = (bf16[4,512,512]{2,1,0:T(8,128)(2,1)}, bf16[4,512,512]{2,1,0:T(8,128)(2,1)}) custom-call(s32[64]{0:T(128)} %reshape.14.slots, bf16[2,512,512]{2,1,0:T(8,128)(2,1)} %get-tuple-element.12.refs_0_.refs_8_, bf16[2,512,512]{2,1,0:T(8,128)(2,1)} %copy-done, bf16[2,512,512]{2,1,0:T(8,128)(2,1)} %copy-done.1, ...), custom_call_target="tpu_custom_call" | custom-call | flops 67108864 | bytes 29360128 | tf_op jit(solution)/shard_map/home/pallas_call | solution.py:157
  263.4 12.9 %density.2.refs_0_ = f32[4,2,512,512]{3,2,1,0:T(8,128)} custom-call(bf16[4,2,2,512,512]{4,3,2,1,0:T(8,128)(2,1)} %g_ref.7, f32[4,2,512]{2,1,0:T(2,128)} %gamma_ref.7, bf16[4,512,512]{2,1,0:T(8,128)(2,1)} %get-tuple-element.16.x_ref, bf16[4,512,512]{2,1,0:T(8,128)(2,1)} %get-tuple-element.17.y_ref), custom_call_target="tpu_custom_call" | custom-call | flops 8589934592 | bytes 20971520 | tf_op jit(solution)/shard_map/density/pallas_call | solution.py:266
  276.3 20.9 %home.2 = (bf16[4,512,512]{2,1,0:T(8,128)(2,1)}, bf16[4,512,512]{2,1,0:T(8,128)(2,1)}) custom-call(s32[64]{0:T(128)} %reshape.14.slots, bf16[2,512,512]{2,1,0:T(8,128)(2,1)} %get-tuple-element.10.refs_0_.refs_8_, bf16[2,512,512]{2,1,0:T(8,128)(2,1)} %copy-done.2, bf16[2,512,512]{2,1,0:T(8,128)(2,1)} %collective-permute-done.4.refs_2_.refs_10_, ...), custom_call_target="tpu_custom_call" | custom-call | flops 67108864 | bytes 29360128 | tf_op jit(solution)/shard_map/home/pallas_call | solution.py:157
  297.2 13.4 %density.3 = bf16[4,2,512,512]{3,2,1,0:T(8,128)(2,1)} custom-call(bf16[4,2,2,512,512]{4,3,2,1,0:T(8,128)(2,1)} %g_ref.7, f32[4,2,512]{2,1,0:T(2,128)} %gamma_ref.7, bf16[4,512,512]{2,1,0:T(8,128)(2,1)} %get-tuple-element.14.x_ref, bf16[4,512,512]{2,1,0:T(8,128)(2,1)} %get-tuple-element.15.y_ref, f32[4,2,512,512]{3,2,1,0:T(8,128)} %density.2.refs_0_), custom_call_target="tpu_custom_call" | custom-call | flops 8589934592 | bytes 20971520 | tf_op jit(solution)/shard_map/density/pallas_call | solution.py:266
  310.5 0.0 reduce-scatter.2.cloned.1.call-update
  310.6 0.6 reshape.13.slots
  311.2 19.8 %rows.2.refs_17_ = bf16[16,2,2,128,512]{4,3,2,1,0:T(8,128)(2,1)} custom-call(s32[1]{0:T(128)} %bitcast.mine, s32[256]{0:T(256)} %reshape.13.slots, bf16[2,512,512]{2,1,0:T(8,128)(2,1)} %get-tuple-element.12.refs_0_.refs_8_, bf16[2,512,512]{2,1,0:T(8,128)(2,1)} %copy-done, bf16[2,512,512]{2,1,0:T(8,128)(2,1)} %copy-done.1, ...), custom_call_target="tpu_custom_call" | custom-call | flops 67108864 | bytes 10485760 | tf_op jit(solution)/shard_map/rows/pallas_call | solution.py:221
  331.0 19.8 %rows.3 = bf16[16,2,2,128,512]{4,3,2,1,0:T(8,128)(2,1)} custom-call(s32[1]{0:T(128)} %bitcast.mine, s32[256]{0:T(256)} %reshape.13.slots, bf16[2,512,512]{2,1,0:T(8,128)(2,1)} %get-tuple-element.10.refs_0_.refs_8_, bf16[2,512,512]{2,1,0:T(8,128)(2,1)} %copy-done.2, ...), custom_call_target="tpu_custom_call", output_to_operand_aliasing={{}: (19, {})} | custom-call | flops 67108864 | bytes 10485760 | tf_op jit(solution)/shard_map/rows/pallas_call | solution.py:221
  350.8 48.7 %reduce-scatter.2.cloned.1.call-done = bf16[4,2,64,512]{3,2,1,0:T(8,128)(2,1)} async-done(((bf16[4,2,512,512]{3,2,1,0:T(8,128)(2,1)}), bf16[4,2,64,512]{3,2,1,0:T(8,128)(2,1)}) %reduce-scatter.2.cloned.1.call-update) | async-done | bytes 524304 | tf_op jit(solution)/shard_map/reduce_scatter | solution.py:340
  399.5 1.2 convert_bitcast_fusion
  400.6 1.8 copy.13
  (33 shorter events, 0.1 us)
Async XLA Ops:
  7.2 208.6 %all-gather.3.cloned.1.call-start = ((), (), s32[]{:S(2)}) async-start(), calls=%async_computation.2 | async-start | bytes 10485760 | tf_op jit(solution)/shard_map/all_gather | solution.py:298
  7.9 391.6 %reduce-scatter.2.cloned.1.call-start = ((), (), s32[]{:S(2)}) async-start(), calls=%async_computation.1 | async-start | bytes 4718592 | tf_op jit(solution)/shard_map/reduce_scatter | solution.py:340
  14.7 48.8 %collective-permute-start = (bf16[2,2,512,512]{3,2,1,0:T(8,128)(2,1)}, bf16[2,2,512,512]{3,2,1,0:T(8,128)(2,1)S(1)}, u32[]{:S(2)}, u32[]{:S(2)}) collective-permute-start(bf16[2,2,512,512]{3,2,1,0:T(8,128)(2,1)} %lesser.3), channel_id=1, source_target_pairs={{0,4},{4,0},{8,12},{12,8},{16,20},{20,16},{24,28},{28,24},{1,5},{5... | collective-permute-start | bytes 6291464 | tf_op jit(solution)/shard_map/ppermute | solution.py:309
  17.7 49.9 %copy-start.8 = (s32[4]{0:T(128)S(1)}, s32[4]{0:T(128)}, u32[]{:S(2)}) copy-start(s32[4]{0:T(128)} %param.10) | copy-start | bytes 52
  17.7 49.9 %copy-start.9 = (f32[4]{0:T(128)S(1)}, f32[4]{0:T(128)}, u32[]{:S(2)}) copy-start(f32[4]{0:T(128)} %param.11) | copy-start | bytes 52
  17.7 49.9 %copy-start.10 = (f32[4]{0:T(128)S(1)}, f32[4]{0:T(128)}, u32[]{:S(2)}) copy-start(f32[4]{0:T(128)} %param.12) | copy-start | bytes 52
  24.6 49.1 %collective-permute-start.1 = (bf16[2,2,512,512]{3,2,1,0:T(8,128)(2,1)}, bf16[2,2,512,512]{3,2,1,0:T(8,128)(2,1)S(1)}, u32[]{:S(2)}, u32[]{:S(2)}) collective-permute-start(bf16[2,2,512,512]{3,2,1,0:T(8,128)(2,1)} %lesser.2.keep), channel_id=1, source_target_pairs={{4,12},{8,0},{12,20},{16,8},{20,28},{24,16},{5,13},{9,1},{13,21},{... | collective-permute-start | bytes 6291464 | tf_op jit(solution)/shard_map/ppermute | solution.py:311
  63.5 47.8 %copy-start.4 = (bf16[2,2,512,512]{3,2,1,0:T(8,128)(2,1)}, bf16[2,2,512,512]{3,2,1,0:T(8,128)(2,1)S(1)}, u32[]{:S(2)}) copy-start(bf16[2,2,512,512]{3,2,1,0:T(8,128)(2,1)S(1)} %collective-permute-done.recv) | copy-start | bytes 6291460
  63.5 47.8 %collective-permute-start.2 = (bf16[2,2,512,512]{3,2,1,0:T(8,128)(2,1)S(1)}, bf16[2,2,512,512]{3,2,1,0:T(8,128)(2,1)S(1)}, u32[]{:S(2)}, u32[]{:S(2)}) collective-permute-start(bf16[2,2,512,512]{3,2,1,0:T(8,128)(2,1)S(1)} %collective-permute-done.recv), channel_id=1, source_target_pairs={{0,8},{8,16},{12,4},{16,24},{20,12},{28,20},{1,9},{9,17},{13,5},{1... | collective-permute-start | bytes 6291464 | tf_op jit(solution)/shard_map/ppermute | solution.py:312
  71.4 143.7 %copy-start.7 = (s32[16,16]{1,0:T(8,128)S(1)}, s32[16,16]{1,0:T(8,128)}, u32[]{:S(2)}) copy-start(s32[16,16]{1,0:T(8,128)} %param.13) | copy-start | bytes 3076
  73.7 37.6 %copy-start.5 = (bf16[2,2,512,512]{3,2,1,0:T(8,128)(2,1)}, bf16[2,2,512,512]{3,2,1,0:T(8,128)(2,1)S(1)}, u32[]{:S(2)}) copy-start(bf16[2,2,512,512]{3,2,1,0:T(8,128)(2,1)S(1)} %collective-permute-done.1.kz) | copy-start | bytes 6291460
  111.3 1.3 copy-start.6
  121.9 26.6 %collective-permute-start.10 = (bf16[2,512,512]{2,1,0:T(8,128)(2,1)}, bf16[2,512,512]{2,1,0:T(8,128)(2,1)S(1)}, u32[]{:S(2)}, u32[]{:S(2)}) collective-permute-start(bf16[2,512,512]{2,1,0:T(8,128)(2,1)} %get-tuple-element.13), channel_id=1, source_target_pairs={{0,4},{4,0},{8,12},{12,8},{16,20},{20,16},{24,28},{28,24},{1,5},{5... | collective-permute-start | bytes 3145736 | tf_op jit(solution)/shard_map/ppermute | solution.py:333
  124.3 26.3 %collective-permute-start.11 = (bf16[2,512,512]{2,1,0:T(8,128)(2,1)}, bf16[2,512,512]{2,1,0:T(8,128)(2,1)S(1)}, u32[]{:S(2)}, u32[]{:S(2)}) collective-permute-start(bf16[2,512,512]{2,1,0:T(8,128)(2,1)} %get-tuple-element.12.refs_0_.refs_8_), channel_id=1, source_target_pairs={{0,2},{1,3},{2,0},{3,1},{4,6},{5,7},{6,4},{7,5},{8,10},{9,11},{10,... | collective-permute-start | bytes 3145736 | tf_op jit(solution)/shard_map/ppermute | solution.py:296
  125.8 24.8 %collective-permute-start.13 = (bf16[2,512,512]{2,1,0:T(8,128)(2,1)}, bf16[2,512,512]{2,1,0:T(8,128)(2,1)S(1)}, u32[]{:S(2)}, u32[]{:S(2)}) collective-permute-start(bf16[2,512,512]{2,1,0:T(8,128)(2,1)} %get-tuple-element.12.refs_0_.refs_8_), channel_id=1, source_target_pairs={{0,1},{1,0},{2,3},{3,2},{4,5},{5,4},{6,7},{7,6},{8,9},{9,8},{10,11... | collective-permute-start | bytes 3145736 | tf_op jit(solution)/shard_map/ppermute | solution.py:296
  125.8 42.7 %collective-permute-start.3 = (bf16[2,512,512]{2,1,0:T(8,128)(2,1)}, bf16[2,512,512]{2,1,0:T(8,128)(2,1)S(1)}, u32[]{:S(2)}, u32[]{:S(2)}) collective-permute-start(bf16[2,512,512]{2,1,0:T(8,128)(2,1)} %get-tuple-element.11), channel_id=1, source_target_pairs={{0,4},{4,0},{8,12},{12,8},{16,20},{20,16},{24,28},{28,24},{1,5},{5... | collective-permute-start | bytes 3145736 | tf_op jit(solution)/shard_map/ppermute | solution.py:333
  148.5 80.9 %copy-start = (bf16[2,512,512]{2,1,0:T(8,128)(2,1)}, bf16[2,512,512]{2,1,0:T(8,128)(2,1)S(1)}, u32[]{:S(2)}) copy-start(bf16[2,512,512]{2,1,0:T(8,128)(2,1)S(1)} %collective-permute-done.10.refs_1_.refs_9_) | copy-start | bytes 3145732
  148.5 26.1 %collective-permute-start.12 = (bf16[2,512,512]{2,1,0:T(8,128)(2,1)S(1)}, bf16[2,512,512]{2,1,0:T(8,128)(2,1)}, u32[]{:S(2)}, u32[]{:S(2)}) collective-permute-start(bf16[2,512,512]{2,1,0:T(8,128)(2,1)S(1)} %collective-permute-done.10.refs_1_.refs_9_), channel_id=1, source_target_pairs={{0,2},{1,3},{2,0},{3,1},{4,6},{5,7},{6,4},{7,5},{8,10},{9,11},{10,... | collective-permute-start | bytes 3145736 | tf_op jit(solution)/shard_map/ppermute | solution.py:296
  150.0 47.1 %collective-permute-start.4 = (bf16[2,512,512]{2,1,0:T(8,128)(2,1)}, bf16[2,512,512]{2,1,0:T(8,128)(2,1)}, u32[]{:S(2)}, u32[]{:S(2)}) collective-permute-start(bf16[2,512,512]{2,1,0:T(8,128)(2,1)} %get-tuple-element.10.refs_0_.refs_8_), channel_id=1, source_target_pairs={{0,2},{1,3},{2,0},{3,1},{4,6},{5,7},{6,4},{7,5},{8,10},{9,11},{10,... | collective-permute-start | bytes 3145736 | tf_op jit(solution)/shard_map/ppermute | solution.py:296
  150.5 78.8 %copy-start.1 = (bf16[2,512,512]{2,1,0:T(8,128)(2,1)}, bf16[2,512,512]{2,1,0:T(8,128)(2,1)S(1)}, u32[]{:S(2)}) copy-start(bf16[2,512,512]{2,1,0:T(8,128)(2,1)S(1)} %collective-permute-done.11.refs_2_.refs_10_) | copy-start | bytes 3145732
  150.6 46.6 %collective-permute-start.14 = (bf16[2,512,512]{2,1,0:T(8,128)(2,1)S(1)}, bf16[2,512,512]{2,1,0:T(8,128)(2,1)}, u32[]{:S(2)}, u32[]{:S(2)}) collective-permute-start(bf16[2,512,512]{2,1,0:T(8,128)(2,1)S(1)} %collective-permute-done.10.refs_1_.refs_9_), channel_id=1, source_target_pairs={{0,1},{1,0},{2,3},{3,2},{4,5},{5,4},{6,7},{7,6},{8,9},{9,8},{10,11... | collective-permute-start | bytes 3145736 | tf_op jit(solution)/shard_map/ppermute | solution.py:296
  150.6 24.1 %copy-start.3 = (bf16[2,512,512]{2,1,0:T(8,128)(2,1)}, bf16[2,512,512]{2,1,0:T(8,128)(2,1)S(1)}, u32[]{:S(2)}) copy-start(bf16[2,512,512]{2,1,0:T(8,128)(2,1)S(1)} %collective-permute-done.13.refs_4_.refs_12_) | copy-start | bytes 3145732
  150.6 47.1 %collective-permute-start.15 = (bf16[2,512,512]{2,1,0:T(8,128)(2,1)S(1)}, bf16[2,512,512]{2,1,0:T(8,128)(2,1)}, u32[]{:S(2)}, u32[]{:S(2)}) collective-permute-start(bf16[2,512,512]{2,1,0:T(8,128)(2,1)S(1)} %collective-permute-done.11.refs_2_.refs_10_), channel_id=1, source_target_pairs={{0,1},{1,0},{2,3},{3,2},{4,5},{5,4},{6,7},{7,6},{8,9},{9,8},{10,11... | collective-permute-start | bytes 3145736 | tf_op jit(solution)/shard_map/ppermute | solution.py:296
  168.5 60.9 %copy-start.2 = (bf16[2,512,512]{2,1,0:T(8,128)(2,1)}, bf16[2,512,512]{2,1,0:T(8,128)(2,1)S(1)}, u32[]{:S(2)}) copy-start(bf16[2,512,512]{2,1,0:T(8,128)(2,1)S(1)} %collective-permute-done.3.refs_1_.refs_9_) | copy-start | bytes 3145732
  168.5 46.5 %collective-permute-start.5 = (bf16[2,512,512]{2,1,0:T(8,128)(2,1)S(1)}, bf16[2,512,512]{2,1,0:T(8,128)(2,1)}, u32[]{:S(2)}, u32[]{:S(2)}) collective-permute-start(bf16[2,512,512]{2,1,0:T(8,128)(2,1)S(1)} %collective-permute-done.3.refs_1_.refs_9_), channel_id=1, source_target_pairs={{0,2},{1,3},{2,0},{3,1},{4,6},{5,7},{6,4},{7,5},{8,10},{9,11},{10,... | collective-permute-start | bytes 3145736 | tf_op jit(solution)/shard_map/ppermute | solution.py:296
  174.7 67.9 %collective-permute-start.16 = (bf16[2,512,512]{2,1,0:T(8,128)(2,1)}, bf16[2,512,512]{2,1,0:T(8,128)(2,1)}, u32[]{:S(2)}, u32[]{:S(2)}) collective-permute-start(bf16[2,512,512]{2,1,0:T(8,128)(2,1)} %collective-permute-done.12.refs_3_.refs_11_), channel_id=1, source_target_pairs={{0,1},{1,0},{2,3},{3,2},{4,5},{5,4},{6,7},{7,6},{8,9},{9,8},{10,11... | collective-permute-start | bytes 3145736 | tf_op jit(solution)/shard_map/ppermute | solution.py:296
  197.1 79.1 %collective-permute-start.6 = (bf16[2,512,512]{2,1,0:T(8,128)(2,1)}, bf16[2,512,512]{2,1,0:T(8,128)(2,1)}, u32[]{:S(2)}, u32[]{:S(2)}) collective-permute-start(bf16[2,512,512]{2,1,0:T(8,128)(2,1)} %get-tuple-element.10.refs_0_.refs_8_), channel_id=1, source_target_pairs={{0,1},{1,0},{2,3},{3,2},{4,5},{5,4},{6,7},{7,6},{8,9},{9,8},{10,11... | collective-permute-start | bytes 3145736 | tf_op jit(solution)/shard_map/ppermute | solution.py:296
  197.1 79.1 %collective-permute-start.7 = (bf16[2,512,512]{2,1,0:T(8,128)(2,1)S(1)}, bf16[2,512,512]{2,1,0:T(8,128)(2,1)}, u32[]{:S(2)}, u32[]{:S(2)}) collective-permute-start(bf16[2,512,512]{2,1,0:T(8,128)(2,1)S(1)} %collective-permute-done.3.refs_1_.refs_9_), channel_id=1, source_target_pairs={{0,1},{1,0},{2,3},{3,2},{4,5},{5,4},{6,7},{7,6},{8,9},{9,8},{10,11... | collective-permute-start | bytes 3145736 | tf_op jit(solution)/shard_map/ppermute | solution.py:296
  197.6 78.6 %collective-permute-start.8 = (bf16[2,512,512]{2,1,0:T(8,128)(2,1)}, bf16[2,512,512]{2,1,0:T(8,128)(2,1)}, u32[]{:S(2)}, u32[]{:S(2)}) collective-permute-start(bf16[2,512,512]{2,1,0:T(8,128)(2,1)} %collective-permute-done.4.refs_2_.refs_10_), channel_id=1, source_target_pairs={{0,1},{1,0},{2,3},{3,2},{4,5},{5,4},{6,7},{7,6},{8,9},{9,8},{10,11... | collective-permute-start | bytes 3145736 | tf_op jit(solution)/shard_map/ppermute | solution.py:296
  215.0 61.2 %collective-permute-start.9 = (bf16[2,512,512]{2,1,0:T(8,128)(2,1)}, bf16[2,512,512]{2,1,0:T(8,128)(2,1)}, u32[]{:S(2)}, u32[]{:S(2)}) collective-permute-start(bf16[2,512,512]{2,1,0:T(8,128)(2,1)} %collective-permute-done.5.refs_3_.refs_11_), channel_id=1, source_target_pairs={{0,1},{1,0},{2,3},{3,2},{4,5},{5,4},{6,7},{7,6},{8,9},{9,8},{10,11... | collective-permute-start | bytes 3145736 | tf_op jit(solution)/shard_map/ppermute | solution.py:296
Sparse Core Ops, SparseCore 0:
  9.5 60.9 all-gather.2
  310.7 88.7 reduce-scatter.1
